TPU v7x, 32 devices: a whole 2x2x4 slice. The times are simulated.
32 devices in a mesh: grp: 2 (over y), visit: 4 (over z), tile: 2 (over x), band: 2 (over core).
Axes of the slice: x: 2, y: 2, z: 4, core: 2. Of those that a mesh axis runs over, the one named last changes fastest.
Arguments:
- template: bfloat16 [256, 512], P(('grp', 'tile', 'band'), 'visit'), parts along dimension 0, may hold values from -6 to 6
- images: bfloat16 [8, 128, 512], P(('grp', 'visit'), ('tile', 'band')), parts along dimension 0, may hold values from -6 to 6
- basis_taps: float32 [3, 19], replicated
- psf_taps: float32 [2, 19], replicated
- coeffs: float32 [8, 3, 6], P('grp'), parts along dimension 0, may hold values from -3 to 3
- offsets: int32 [8, 2], P('grp'), parts along dimension 0, may hold values from -8 to 8, as said below
- intersection: int32 [8, 4], P('grp'), parts along dimension 0, may hold values from 0 to 1, as said below
- weights: float32 [8], P('grp'), parts along dimension 0, may hold values from 0.5 to 4
Outputs:
- coadd: float32 [256, 512], P(('grp', 'tile', 'band'), 'visit'), parts along dimension 0
There are 2 independent parts, one for each index of `grp`. A program takes and returns all parts, laid end to end along the dimension named above; an argument that names none is the same for every part. Nothing has to cross between parts.
Inputs may be any that keep to these rules, and one draw needn't show every extreme that they name: `offsets`: some visit has row offset 8 and some visit has column offset -8. `intersection`: every slab is covered by at least one visit.
All inputs are finite; a program needn't handle non-finite values.
Results may differ from a plain program's by a relative error of at most 0.00069.
Values may be sent and summed in bfloat16 or wider, within the bound.
A program may use at most 64 MiB of HBM per device.

v0:
```python
import functools

import jax
import jax.numpy as jnp
from jax import lax
from jax.experimental import pallas as pl
from jax.experimental.pallas import tpu as pltpu
from jax.sharding import PartitionSpec as P

BASES = 3
TAPS = 19
RADIUS = TAPS // 2
SHIFT = 8
LANES = 128
WIDE = 2 * LANES
HALO = 16
F32 = jnp.float32
BF16 = jnp.bfloat16


def split(x):
    high = x.astype(BF16)
    return high, (x - high.astype(F32)).astype(BF16)


def mm(a, b):
    return jnp.dot(a, b, preferred_element_type=F32)


def mm_split(a, b):
    a_high, a_low = split(a)
    b_high, b_low = split(b)
    return mm(a_high, b_high) + (mm(a_high, b_low) + mm(a_low, b_high))


def band(taps, row, rows, width, start, flip):
    lane = lax.broadcasted_iota(jnp.int32, (8, width), 1)
    line = jnp.zeros((8, width), F32)
    for t in range(TAPS):
        d = (RADIUS - t) if flip else (t - RADIUS)
        line = jnp.where(lane == d % width, taps[row, t], line)
    full = jnp.broadcast_to(line[:1], (rows, width))
    return pltpu.roll(full, start % width, 1, stride=1, stride_axis=0)


def pack(block, first):
    groups = block.shape[0] // 8
    width = LANES // groups
    lane = lax.broadcasted_iota(jnp.int32, (8, LANES), 1)
    packed = None
    for g in range(groups):
        part = pltpu.roll(block[8 * g:8 * g + 8], (width * g - first) % LANES, 1)
        packed = part if packed is None else jnp.where(lane < width * g, packed, part)
    return packed.astype(BF16)


def unpack(packed, first, groups, count):
    width = LANES // count
    packed = packed.astype(F32)
    return [pltpu.roll(packed, (first - width * g) % LANES, 1) for g in groups]


def kernel(
    sizes,
    template, images, *small,
):
    small, (
        out,
        image, basis_taps, psf_taps, coeffs, offsets, cover, weights,
        tiles, windows, packs, tile_packs, tile_sides, cols_high, cols_low,
        loaded, sent_tiles, got_tiles, sent_windows, got_windows,
    ) = small[:6], small[6:]
    visits, slabs, bands = sizes
    slab_rows = template.shape[0]
    groups, halo = slab_rows // 8, HALO // 8
    main = 1 + halo
    below_main = main + groups + 1
    patch_rows, patch_cols = slab_rows * slabs, images.shape[3]
    me = lax.axis_index("visit")
    slab = lax.axis_index("tile") * bands + lax.axis_index("band")

    def place(visit, row):
        return {"visit": visit, "tile": lax.div(row, bands), "band": lax.rem(row, bands)}

    above, below = slab > 0, slab < slabs - 1

    loads = [
        pltpu.make_async_copy(source, target, loaded.at[i])
        for i, (source, target) in enumerate(
            zip(
                (images.at[0], template, *small),
                (image, tiles.at[1], basis_taps, psf_taps, coeffs, offsets, cover, weights),
            )
        )
    ]
    for load in loads[:2]:
        load.start()

    barrier = pltpu.get_barrier_semaphore()
    for k in range(visits):
        other = lax.rem(me + k, visits)
        if k > 0:
            pl.semaphore_signal(barrier, 1, device_id=place(other, slab))
        pl.when(above)(lambda: pl.semaphore_signal(barrier, 1, device_id=place(other, slab - 1)))
        pl.when(below)(lambda: pl.semaphore_signal(barrier, 1, device_id=place(other, slab + 1)))

    for load in loads[2:]:
        load.start()

    for dr in (-1, 0, 1):
        for dc in (-1, 0, 1):
            if (dr, dc) == (0, 0):
                continue
            missing = jnp.logical_or(
                jnp.logical_or(slab + dr < 0, slab + dr >= slabs),
                jnp.logical_or(me + dc < 0, me + dc >= visits),
            )

            def blank(dr=dr, dc=dc):
                if dc == 0:
                    tiles[1 + dr] = jnp.zeros((slab_rows, LANES), BF16)
                else:
                    tile_sides[(1 + dc) // 2, 1 + dr] = jnp.zeros((8, LANES), BF16)

            pl.when(missing)(blank)

    loads[1].wait()
    own = tiles[1].astype(F32)
    tile_packs[0] = pack(own, 0)
    tile_packs[1] = pack(own, LANES - LANES // groups)
    loads[0].wait()
    lane = lax.broadcasted_iota(jnp.int32, (slab_rows, LANES), 1)
    blocks = [image[:, :, b * LANES:(b + 1) * LANES].astype(F32).reshape(slab_rows, LANES) for b in range(visits)]
    for b in range(visits):
        right, left = blocks[min(b + 1, visits - 1)], blocks[max(b - 1, 0)]
        packs[b] = pack(jnp.where(lane < LANES // 2, right, left), -LANES // groups // 2)
    count = visits - 1 + visits * (above.astype(jnp.int32) + below.astype(jnp.int32))
    pl.semaphore_wait(barrier, count)

    def tile_copy(dr, dc):
        if dc == 0:
            source, target = template, tiles.at[1 - dr]
        else:
            source, target = tile_packs.at[(1 + dc) // 2], tile_sides.at[(1 - dc) // 2, 1 - dr]
        return pltpu.make_async_remote_copy(
            src_ref=source,
            dst_ref=target,
            send_sem=sent_tiles.at[1 + dc],
            recv_sem=got_tiles.at[1 - dc],
            device_id=place(me + dc, slab + dr),
        )

    def for_tiles(act, columns=(0, -1, 1)):
        for dc in columns:
            for dr in (-1, 1) if dc == 0 else (0, -1, 1):
                there = jnp.logical_and(
                    jnp.logical_and(slab + dr >= 0, slab + dr < slabs),
                    jnp.logical_and(me + dc >= 0, me + dc < visits),
                )
                pl.when(there)(lambda dr=dr, dc=dc: act(dr, dc))

    def window_copy(other, dr):
        if dr == 0:
            first, height, target = 0, groups, main
        elif dr < 0:
            first, height, target = 0, halo, below_main
        else:
            first, height, target = groups - halo, halo, 1
        return pltpu.make_async_remote_copy(
            src_ref=images.at[0, pl.ds(first, height), :, pl.ds(pl.multiple_of(other * LANES, LANES), LANES)],
            dst_ref=windows.at[me, pl.ds(target, height)],
            send_sem=sent_windows.at[other],
            recv_sem=got_windows.at[me],
            device_id=place(other, slab + dr),
        )

    def side_copy(other, dr):
        return pltpu.make_async_remote_copy(
            src_ref=packs.at[other],
            dst_ref=windows.at[me, (below_main + halo, main + groups, 0)[1 + dr]],
            send_sem=sent_windows.at[other],
            recv_sem=got_windows.at[me],
            device_id=place(other, slab + dr),
        )

    beside = above.astype(jnp.int32) + below.astype(jnp.int32)

    def await_bytes(ref, size, sem):
        if size > 0:
            part = ref.at[pl.ds(0, size)]
            pltpu.make_async_copy(part, part, sem).wait()

    def await_windows(sems, other):
        for near in range(3):
            for own in (False, True):
                size = near * (halo + 1) + (0 if own else groups + 1)
                pl.when(jnp.logical_and(beside == near, (other == me) == own))(
                    lambda size=size: await_bytes(windows.at[other], size, sems.at[other])
                )

    def await_tiles(sems):
        for dc in (0, -1, 1):
            there = jnp.logical_and(me + dc >= 0, me + dc < visits)
            for near in range(3):
                ref, size = (tiles, near) if dc == 0 else (tile_sides.at[0], near + 1)
                pl.when(jnp.logical_and(beside == near, there))(
                    lambda ref=ref, size=size, dc=dc: await_bytes(ref, size, sems.at[1 + dc])
                )

    def for_windows(other, act):
        pl.when(other != me)(lambda: act(other, 0))
        pl.when(above)(lambda: act(other, -1))
        pl.when(below)(lambda: act(other, 1))

    for_tiles(lambda dr, dc: tile_copy(dr, dc).start(), (0,))
    for_tiles(lambda dr, dc: tile_copy(dr, dc).start(), (-1, 1))
    def send_window(other, dr):
        side_copy(other, dr).start()
        window_copy(other, dr).start()

    for b in range(visits):
        for_windows(jnp.int32(b), send_window)


    windows[me, main:main + groups] = image[:, :, pl.ds(pl.multiple_of(me * LANES, LANES), LANES)]
    windows[me, main + groups] = packs[me]
    for load in loads[2:]:
        load.wait()

    out_rows = slab_rows + 2 * (HALO + SHIFT)
    in_rows = 3 * slab_rows
    first = slab_rows - HALO - SHIFT
    rows_parts = []
    for b in range(BASES):
        rows_parts.append(split(band(basis_taps, b, out_rows, LANES, first, False)[:, :in_rows]))
        high, low = split(band(basis_taps, b, WIDE, WIDE, 0, True))
        cols_high[b], cols_low[b] = high, low
    psf_rows = band(psf_taps, 0, slab_rows, LANES, HALO, False)[:, :slab_rows + 2 * HALO]
    high, low = split(band(psf_taps, 1, WIDE, WIDE, 0, True)[:, :LANES])
    cols_high[BASES, :, :LANES], cols_low[BASES, :, :LANES] = high, low

    column = lax.broadcasted_iota(jnp.int32, (8, WIDE), 1)
    column = jnp.where(column < WIDE - LANES // 2, column, column - WIDE) + me * LANES
    inside_cols = jnp.logical_and(column >= 0, column < patch_cols)[:1]
    column = column.astype(F32)[:1]
    row = lax.broadcasted_iota(jnp.int32, (out_rows, LANES), 0) + (slab * slab_rows - HALO - SHIFT)
    inside_rows = jnp.logical_and(row >= 0, row < patch_rows)
    row = row.astype(F32)

    await_tiles(got_tiles)
    lane = lax.broadcasted_iota(jnp.int32, (in_rows, LANES), 1)
    every, width = range(groups), LANES // groups
    centre = tiles[...].astype(F32).reshape(in_rows, LANES)
    right, left = [], []
    for part in range(3):
        left += unpack(tile_sides[0, part], LANES - width, every, groups)
        right += unpack(tile_sides[1, part], 0, every, groups)
    right, left = jnp.concatenate(right, axis=0), jnp.concatenate(left, axis=0)
    field = jnp.concatenate([centre, jnp.where(lane < LANES // 2, right, left)], axis=1).astype(BF16)
    planes = []
    inside = jnp.logical_and(jnp.concatenate([inside_rows, inside_rows], axis=1), inside_cols)
    for b in range(BASES):
        high, low = rows_parts[b]
        passed = mm(high, field) + mm(low, field)
        high, low = split(passed)
        plane = mm(high, cols_high[b]) + (mm(high, cols_low[b]) + mm(low, cols_high[b]))
        planes.append(jnp.where(inside, plane, 0.0).astype(BF16).astype(F32))

    window_rows = slab_rows + 2 * HALO
    denominator = jnp.float32(0)
    total = jnp.zeros((window_rows, WIDE), F32)
    models = []
    for k in range(visits):
        source = lax.rem(me + k, visits)
        dy, dx = offsets[0, source], offsets[1, source]
        u = (column - dx.astype(F32) + 0.5) * (2.0 / patch_cols) - 1.0
        w = (row - dy.astype(F32) + 0.5) * (2.0 / patch_rows) - 1.0
        model = None
        for b in range(BASES):
            c = [coeffs[b, source, q] for q in range(6)]
            still = c[0] + w * (c[2] + c[5] * w)
            slope = c[1] + c[4] * w
            both = lambda x: jnp.concatenate([x, x], axis=1)
            term = (both(still) + u * (both(slope) + c[3] * u)) * planes[b]
            model = term if model is None else model + term
        moved = pltpu.roll(model, out_rows - SHIFT - dy, 0)[:window_rows]
        models.append(pltpu.roll(moved, jnp.where(dx > 0, WIDE - dx, -dx), 1))

    for k in range(visits):
        source = lax.rem(me + k, visits)
        if k == visits - 1:
            await_tiles(sent_tiles)
            for b in range(visits):
                await_windows(sent_windows, jnp.int32(b))
        await_windows(got_windows, source)
        window = windows[source].astype(F32)
        columns = []
        for part, chosen in (
            (0, every[-halo:]), (main + groups, every), (below_main + halo, every[:halo])
        ):
            columns += unpack(windows[source, part], -(width // 2), chosen, groups)
        blocks = [window[1:main + groups], window[below_main:below_main + halo]]
        seen = jnp.concatenate(
            [
                jnp.concatenate(blocks, axis=0).reshape(window_rows, LANES),
                jnp.concatenate(columns, axis=0),
            ],
            axis=1,
        )
        difference = (seen - models[k]).astype(BF16).astype(F32)
        weight = weights[source] * cover[source, slab].astype(F32)
        denominator = denominator + weight
        total = total + weight * difference

    y = lax.broadcasted_iota(jnp.int32, (window_rows, WIDE), 0) + (slab * slab_rows - HALO)
    total = jnp.where(
        jnp.logical_and(jnp.logical_and(y >= 0, y < patch_rows), inside_cols), total, 0.0
    )
    passed = mm_split(psf_rows, total)
    high, low = split(passed)
    psf_high, psf_low = cols_high[BASES, :, :LANES], cols_low[BASES, :, :LANES]
    filtered = mm(high, psf_high) + (mm(high, psf_low) + mm(low, psf_high))
    out[...] = filtered / jnp.full(filtered.shape, denominator, F32)


def solution(mesh):
    visits, bands = mesh.shape["visit"], mesh.shape["band"]
    slabs = mesh.shape["tile"] * bands

    def shards(template, images, basis_taps, psf_taps, coeffs, offsets, cover, weights):
        slab_rows = template.shape[0]
        images = images.reshape(images.shape[0], slab_rows // 8, 8, images.shape[2])
        vmem = pl.BlockSpec(memory_space=pltpu.VMEM)
        small = (
            basis_taps, psf_taps, coeffs.transpose(1, 0, 2), offsets.transpose(1, 0), cover, weights
        )
        return pl.pallas_call(
            functools.partial(kernel, (visits, slabs, bands)),
            out_shape=pltpu.VMEM(template.shape, F32),
            in_specs=[pl.BlockSpec(memory_space=pl.ANY)] * 8,
            out_specs=vmem,
            scratch_shapes=[
                pltpu.VMEM(images.shape[1:], BF16),
                *[pltpu.SMEM(x.shape, x.dtype) for x in small],
                pltpu.VMEM((3, slab_rows, LANES), BF16),
                pltpu.VMEM((visits, (slab_rows + 2 * HALO) // 8 + 3, 8, LANES), BF16),
                pltpu.VMEM((visits, 8, LANES), BF16),
                pltpu.VMEM((2, 8, LANES), BF16),
                pltpu.VMEM((2, 3, 8, LANES), BF16),
                pltpu.VMEM((BASES + 1, WIDE, WIDE), BF16),
                pltpu.VMEM((BASES + 1, WIDE, WIDE), BF16),
                pltpu.SemaphoreType.DMA((8,)),
                pltpu.SemaphoreType.DMA((3,)),
                pltpu.SemaphoreType.DMA((3,)),
                pltpu.SemaphoreType.DMA((visits,)),
                pltpu.SemaphoreType.DMA((visits,)),
            ],
            compiler_params=pltpu.CompilerParams(collective_id=0, has_side_effects=True),
            name="coadd",
        )(template, images, *small)

    placed = (
        P(("grp", "tile", "band"), "visit"),
        P(("grp", "visit"), ("tile", "band"), None),
        P(),
        P(),
        P("grp", None, None),
        P("grp", None),
        P("grp", None),
        P("grp"),
    )
    return jax.shard_map(
        shards,
        mesh=mesh,
        in_specs=placed,
        out_specs=P(("grp", "tile", "band"), "visit"),
        check_vma=False,
    )
```

profile of v0, /device:TPU:1, one launch (start us, length us, event | category | flops | bytes accessed | tf_op | source)
XLA Modules:
  0.0 10.4 jit_solution(16713342971919146838)
XLA Ops:
  0.0 9.8 %coadd.1 = f32[32,128]{1,0:T(8,128)S(1)} custom-call(bf16[32,128]{1,0:T(8,128)(2,1)} %template.1, bf16[1,4,8,512]{3,2,1,0:T(8,128)(2,1)} %bitcast.3, f32[3,19]{1,0:T(4,128)} %small_0_.1, f32[2,19]{1,0:T(2,128)} %small_1_.1, f32[3,4,6]{2,1,0:T(4,128)} %bitcast.4, s32[2,4]{1,0:T(2,128)} %bitcast.5, s32[4,4]{1,0:T(4,128)} %small_4_.1, f32[4]{0:T(128)} %small_5_.1), custom_call_target="tpu_custom_call" | custom-call | tf_op jit(solution)/shard_map/coadd/pallas_call | solution.py:337
  9.8 0.6 %copy.10 = f32[32,128]{1,0:T(8,128)} copy(f32[32,128]{1,0:T(8,128)S(1)} %coadd.1) | data formatting | bytes 32768
where the time goes:
time: 10.6 us; the launch traced here: 10.4 us
  Pallas kernels  9.82 us (93%)
  local copies, waits for them, and re-layouts  0.61 us (6%)
    pallas_call x1, Pallas kernels, shards(): pl.pallas_call(functools.partial(kernel, (visits, slabs, bands)), out_sha...  9.82 us
    unnamed x1, local copies, waits for them, and re-layouts  0.61 us

commit v1 on v0

--- a/solution.py
+++ b/solution.py
@@ -68,7 +68,7 @@
         out,
         image, basis_taps, psf_taps, coeffs, offsets, cover, weights,
         tiles, windows, packs, tile_packs, tile_sides, cols_high, cols_low,
-        loaded, sent_tiles, got_tiles, sent_windows, got_windows,
+        loaded, sent_tiles, got_tiles, sent_windows, got_windows, ready,
     ) = small[:6], small[6:]
     visits, slabs, bands = sizes
     slab_rows = template.shape[0]
@@ -96,13 +96,16 @@
     for load in loads[:2]:
         load.start()
 
+    beside = above.astype(jnp.int32) + below.astype(jnp.int32)
+
+    def greet(semaphore, other, beyond, row):
+        pl.semaphore_signal(semaphore, 1, device_id=place(other, slab))
+        pl.when(beyond)(lambda: pl.semaphore_signal(semaphore, 1, device_id=place(other, row)))
+
     barrier = pltpu.get_barrier_semaphore()
-    for k in range(visits):
-        other = lax.rem(me + k, visits)
-        if k > 0:
-            pl.semaphore_signal(barrier, 1, device_id=place(other, slab))
-        pl.when(above)(lambda: pl.semaphore_signal(barrier, 1, device_id=place(other, slab - 1)))
-        pl.when(below)(lambda: pl.semaphore_signal(barrier, 1, device_id=place(other, slab + 1)))
+    pl.when(below)(lambda: pl.semaphore_signal(barrier, 1, device_id=place(me, slab + 1)))
+    for b in range(visits):
+        pl.when(me < b)(lambda b=b: greet(barrier, jnp.int32(b), below, slab + 1))
 
     for load in loads[2:]:
         load.start()
@@ -123,6 +126,12 @@
                     tile_sides[(1 + dc) // 2, 1 + dr] = jnp.zeros((8, LANES), BF16)
 
             pl.when(missing)(blank)
+
+    ahead = me * (1 + above.astype(jnp.int32)) + above.astype(jnp.int32)
+    pl.when(ahead > 0)(lambda: pl.semaphore_wait(barrier, ahead))
+    pl.when(above)(lambda: pl.semaphore_signal(ready.at[me], 1, device_id=place(me, slab - 1)))
+    for b in range(visits):
+        pl.when(me > b)(lambda b=b: greet(ready.at[me], jnp.int32(b), above, slab - 1))
 
     loads[1].wait()
     own = tiles[1].astype(F32)
@@ -134,12 +143,10 @@
     for b in range(visits):
         right, left = blocks[min(b + 1, visits - 1)], blocks[max(b - 1, 0)]
         packs[b] = pack(jnp.where(lane < LANES // 2, right, left), -LANES // groups // 2)
-    count = visits - 1 + visits * (above.astype(jnp.int32) + below.astype(jnp.int32))
-    pl.semaphore_wait(barrier, count)
 
     def tile_copy(dr, dc):
         if dc == 0:
-            source, target = template, tiles.at[1 - dr]
+            source, target = tiles.at[1], tiles.at[1 - dr]
         else:
             source, target = tile_packs.at[(1 + dc) // 2], tile_sides.at[(1 - dc) // 2, 1 - dr]
         return pltpu.make_async_remote_copy(
@@ -150,15 +157,6 @@
             device_id=place(me + dc, slab + dr),
         )
 
-    def for_tiles(act, columns=(0, -1, 1)):
-        for dc in columns:
-            for dr in (-1, 1) if dc == 0 else (0, -1, 1):
-                there = jnp.logical_and(
-                    jnp.logical_and(slab + dr >= 0, slab + dr < slabs),
-                    jnp.logical_and(me + dc >= 0, me + dc < visits),
-                )
-                pl.when(there)(lambda dr=dr, dc=dc: act(dr, dc))
-
     def window_copy(other, dr):
         if dr == 0:
             first, height, target = 0, groups, main
@@ -167,7 +165,7 @@
         else:
             first, height, target = groups - halo, halo, 1
         return pltpu.make_async_remote_copy(
-            src_ref=images.at[0, pl.ds(first, height), :, pl.ds(pl.multiple_of(other * LANES, LANES), LANES)],
+            src_ref=image.at[pl.ds(first, height), :, pl.ds(pl.multiple_of(other * LANES, LANES), LANES)],
             dst_ref=windows.at[me, pl.ds(target, height)],
             send_sem=sent_windows.at[other],
             recv_sem=got_windows.at[me],
@@ -183,7 +181,12 @@
             device_id=place(other, slab + dr),
         )
 
-    beside = above.astype(jnp.int32) + below.astype(jnp.int32)
+    def nearest(k):
+        both = 2 * jnp.minimum(me, visits - 1 - me)
+        paired = me + ((k + 1) // 2) * (1 if k % 2 == 0 else -1)
+        rest = jnp.where(2 * me < visits - 1, k, visits - 1 - k)
+        return jnp.where(k <= both, paired, rest)
+
 
     def await_bytes(ref, size, sem):
         if size > 0:
@@ -207,20 +210,39 @@
                     lambda ref=ref, size=size, dc=dc: await_bytes(ref, size, sems.at[1 + dc])
                 )
 
-    def for_windows(other, act):
-        pl.when(other != me)(lambda: act(other, 0))
-        pl.when(above)(lambda: act(other, -1))
-        pl.when(below)(lambda: act(other, 1))
-
-    for_tiles(lambda dr, dc: tile_copy(dr, dc).start(), (0,))
-    for_tiles(lambda dr, dc: tile_copy(dr, dc).start(), (-1, 1))
     def send_window(other, dr):
         side_copy(other, dr).start()
         window_copy(other, dr).start()
 
-    for b in range(visits):
-        for_windows(jnp.int32(b), send_window)
-
+    def send_windows(other, rows=(0, -1, 1)):
+        for dr in rows:
+            if dr == 0:
+                send_window(other, 0)
+            else:
+                pl.when(above if dr < 0 else below)(lambda dr=dr: send_window(other, dr))
+
+    def send_tiles(dc, rows=(0, -1, 1)):
+        for dr in rows:
+            if dr == 0:
+                tile_copy(0, dc).start()
+            else:
+                pl.when(above if dr < 0 else below)(lambda dr=dr: tile_copy(dr, dc).start())
+
+    def send_row(dr):
+        tile_copy(dr, 0).start()
+        send_window(me, dr)
+
+    def await_ready(other):
+        pl.semaphore_wait(ready.at[other], 1 + below.astype(jnp.int32))
+
+    def send_ahead(rows):
+        for b in range(visits - 2):
+            pl.when(me > b + 1)(lambda b=b: send_windows(jnp.int32(b), rows))
+        pl.when(me > 0)(lambda: send_tiles(-1, rows))
+        pl.when(me > 0)(lambda: send_windows(me - 1, rows))
+
+    pl.when(above)(lambda: send_row(-1))
+    send_ahead((-1, 0))
 
     windows[me, main:main + groups] = image[:, :, pl.ds(pl.multiple_of(me * LANES, LANES), LANES)]
     windows[me, main + groups] = packs[me]
@@ -246,6 +268,29 @@
     row = lax.broadcasted_iota(jnp.int32, (out_rows, LANES), 0) + (slab * slab_rows - HALO - SHIFT)
     inside_rows = jnp.logical_and(row >= 0, row < patch_rows)
     row = row.astype(F32)
+
+    def send_below():
+        pl.semaphore_wait(ready.at[me], 1)
+        send_row(1)
+        send_ahead((1,))
+
+    pl.when(below)(send_below)
+
+    def send_next():
+        await_ready(me + 1)
+        send_tiles(1)
+        send_windows(me + 1)
+
+    pl.when(me < visits - 1)(send_next)
+
+    def send_far(other):
+        await_ready(other)
+        send_windows(other)
+
+    pl.when(me + 2 < visits)(lambda: send_far(me + 2))
+
+    for b in range(3, visits):
+        pl.when(me + 2 < b)(lambda b=b: send_far(jnp.int32(b)))
 
     await_tiles(got_tiles)
     lane = lax.broadcasted_iota(jnp.int32, (in_rows, LANES), 1)
@@ -271,7 +316,7 @@
     total = jnp.zeros((window_rows, WIDE), F32)
     models = []
     for k in range(visits):
-        source = lax.rem(me + k, visits)
+        source = nearest(k)
         dy, dx = offsets[0, source], offsets[1, source]
         u = (column - dx.astype(F32) + 0.5) * (2.0 / patch_cols) - 1.0
         w = (row - dy.astype(F32) + 0.5) * (2.0 / patch_rows) - 1.0
@@ -287,11 +332,7 @@
         models.append(pltpu.roll(moved, jnp.where(dx > 0, WIDE - dx, -dx), 1))
 
     for k in range(visits):
-        source = lax.rem(me + k, visits)
-        if k == visits - 1:
-            await_tiles(sent_tiles)
-            for b in range(visits):
-                await_windows(sent_windows, jnp.int32(b))
+        source = nearest(k)
         await_windows(got_windows, source)
         window = windows[source].astype(F32)
         columns = []
@@ -321,6 +362,9 @@
     psf_high, psf_low = cols_high[BASES, :, :LANES], cols_low[BASES, :, :LANES]
     filtered = mm(high, psf_high) + (mm(high, psf_low) + mm(low, psf_high))
     out[...] = filtered / jnp.full(filtered.shape, denominator, F32)
+    await_tiles(sent_tiles)
+    for b in range(visits):
+        await_windows(sent_windows, jnp.int32(b))
 
 
 def solution(mesh):
@@ -354,6 +398,7 @@
                 pltpu.SemaphoreType.DMA((3,)),
                 pltpu.SemaphoreType.DMA((visits,)),
                 pltpu.SemaphoreType.DMA((visits,)),
+                pltpu.SemaphoreType.REGULAR((visits,)),
             ],
             compiler_params=pltpu.CompilerParams(collective_id=0, has_side_effects=True),
             name="coadd",

time: 10.6 us -> 9.27 us (0.87)
  Pallas kernels: 9.82 us -> 8.47 us
    pallas_call x1, Pallas kernels: 9.82 us -> 8.47 us  [shards(): pl.pallas_call(functools.partial(kernel, (visits, slabs, bands)), out_sha...]
where the time goes in v1:
time: 9.27 us; the launch traced here: 9.09 us
  Pallas kernels  8.47 us (91%)
  local copies, waits for them, and re-layouts  0.61 us (7%)
    pallas_call x1, Pallas kernels, shards(): pl.pallas_call(functools.partial(kernel, (visits, slabs, bands)), out_sha...  8.47 us
    unnamed x1, local copies, waits for them, and re-layouts  0.61 us

profile of v1, /device:TPU:1, one launch (start us, length us, event | category | flops | bytes accessed | tf_op | source)
XLA Modules:
  0.0 9.1 jit_solution(14687097110752302286)
XLA Ops:
  0.0 8.5 %coadd.1 = f32[32,128]{1,0:T(8,128)S(1)} custom-call(bf16[32,128]{1,0:T(8,128)(2,1)} %template.1, bf16[1,4,8,512]{3,2,1,0:T(8,128)(2,1)} %bitcast.3, f32[3,19]{1,0:T(4,128)} %small_0_.1, f32[2,19]{1,0:T(2,128)} %small_1_.1, f32[3,4,6]{2,1,0:T(4,128)} %bitcast.4, s32[2,4]{1,0:T(2,128)} %bitcast.5, s32[4,4]{1,0:T(4,128)} %small_4_.1, f32[4]{0:T(128)} %small_5_.1), custom_call_target="tpu_custom_call" | custom-call | tf_op jit(solution)/shard_map/coadd/pallas_call | solution.py:381
  8.5 0.6 %copy.10 = f32[32,128]{1,0:T(8,128)} copy(f32[32,128]{1,0:T(8,128)S(1)} %coadd.1) | data formatting | bytes 32768

commit v2 on v1

--- a/solution.py
+++ b/solution.py
@@ -68,7 +68,7 @@
         out,
         image, basis_taps, psf_taps, coeffs, offsets, cover, weights,
         tiles, windows, packs, tile_packs, tile_sides, cols_high, cols_low,
-        loaded, sent_tiles, got_tiles, sent_windows, got_windows, ready,
+        loaded, counted, sent, got_tiles, got_windows, ready,
     ) = small[:6], small[6:]
     visits, slabs, bands = sizes
     slab_rows = template.shape[0]
@@ -85,7 +85,7 @@
     above, below = slab > 0, slab < slabs - 1
 
     loads = [
-        pltpu.make_async_copy(source, target, loaded.at[i])
+        pltpu.make_async_copy(source, target, loaded.at[min(i // 2, 1)])
         for i, (source, target) in enumerate(
             zip(
                 (images.at[0], template, *small),
@@ -133,16 +133,12 @@
     for b in range(visits):
         pl.when(me > b)(lambda b=b: greet(ready.at[me], jnp.int32(b), above, slab - 1))
 
-    loads[1].wait()
-    own = tiles[1].astype(F32)
-    tile_packs[0] = pack(own, 0)
-    tile_packs[1] = pack(own, LANES - LANES // groups)
-    loads[0].wait()
-    lane = lax.broadcasted_iota(jnp.int32, (slab_rows, LANES), 1)
-    blocks = [image[:, :, b * LANES:(b + 1) * LANES].astype(F32).reshape(slab_rows, LANES) for b in range(visits)]
-    for b in range(visits):
-        right, left = blocks[min(b + 1, visits - 1)], blocks[max(b - 1, 0)]
-        packs[b] = pack(jnp.where(lane < LANES // 2, right, left), -LANES // groups // 2)
+    def await_bytes(ref, size, sem):
+        if size > 0:
+            part = ref.at[pl.ds(0, size)]
+            pltpu.make_async_copy(part, part, sem).wait()
+
+    await_bytes(counted, groups * (1 + visits), loaded.at[0])
 
     def tile_copy(dr, dc):
         if dc == 0:
@@ -152,8 +148,8 @@
         return pltpu.make_async_remote_copy(
             src_ref=source,
             dst_ref=target,
-            send_sem=sent_tiles.at[1 + dc],
-            recv_sem=got_tiles.at[1 - dc],
+            send_sem=sent.at[0],
+            recv_sem=got_tiles.at[0],
             device_id=place(me + dc, slab + dr),
         )
 
@@ -167,7 +163,7 @@
         return pltpu.make_async_remote_copy(
             src_ref=image.at[pl.ds(first, height), :, pl.ds(pl.multiple_of(other * LANES, LANES), LANES)],
             dst_ref=windows.at[me, pl.ds(target, height)],
-            send_sem=sent_windows.at[other],
+            send_sem=sent.at[0],
             recv_sem=got_windows.at[me],
             device_id=place(other, slab + dr),
         )
@@ -176,7 +172,7 @@
         return pltpu.make_async_remote_copy(
             src_ref=packs.at[other],
             dst_ref=windows.at[me, (below_main + halo, main + groups, 0)[1 + dr]],
-            send_sem=sent_windows.at[other],
+            send_sem=sent.at[0],
             recv_sem=got_windows.at[me],
             device_id=place(other, slab + dr),
         )
@@ -187,11 +183,6 @@
         rest = jnp.where(2 * me < visits - 1, k, visits - 1 - k)
         return jnp.where(k <= both, paired, rest)
 
-
-    def await_bytes(ref, size, sem):
-        if size > 0:
-            part = ref.at[pl.ds(0, size)]
-            pltpu.make_async_copy(part, part, sem).wait()
 
     def await_windows(sems, other):
         for near in range(3):
@@ -201,14 +192,19 @@
                     lambda size=size: await_bytes(windows.at[other], size, sems.at[other])
                 )
 
-    def await_tiles(sems):
-        for dc in (0, -1, 1):
-            there = jnp.logical_and(me + dc >= 0, me + dc < visits)
-            for near in range(3):
-                ref, size = (tiles, near) if dc == 0 else (tile_sides.at[0], near + 1)
-                pl.when(jnp.logical_and(beside == near, there))(
-                    lambda ref=ref, size=size, dc=dc: await_bytes(ref, size, sems.at[1 + dc])
+    def await_blocks(sem, blocks):
+        sides = (me > 0).astype(jnp.int32) + (me < visits - 1).astype(jnp.int32)
+        for near in range(3):
+            for wide in range(3):
+                pl.when(jnp.logical_and(beside == near, sides == wide))(
+                    lambda size=blocks(near, wide): await_bytes(counted, size, sem)
                 )
+
+    def tile_blocks(near, wide):
+        return near * groups + wide * (1 + near)
+
+    def sent_blocks(near, wide):
+        return tile_blocks(near, wide) + (visits - 1) * (groups + 1) + visits * near * (halo + 1)
 
     def send_window(other, dr):
         side_copy(other, dr).start()
@@ -235,14 +231,26 @@
     def await_ready(other):
         pl.semaphore_wait(ready.at[other], 1 + below.astype(jnp.int32))
 
+    def send_next_ahead(rows):
+        pl.when(me > 0)(lambda: send_tiles(-1, rows))
+        pl.when(me > 0)(lambda: send_windows(me - 1, rows))
+
     def send_ahead(rows):
         for b in range(visits - 2):
             pl.when(me > b + 1)(lambda b=b: send_windows(jnp.int32(b), rows))
-        pl.when(me > 0)(lambda: send_tiles(-1, rows))
-        pl.when(me > 0)(lambda: send_windows(me - 1, rows))
-
+        send_next_ahead(rows)
+
+    lane = lax.broadcasted_iota(jnp.int32, (slab_rows, LANES), 1)
+    blocks = [image[:, :, b * LANES:(b + 1) * LANES].astype(F32).reshape(slab_rows, LANES) for b in range(visits)]
+    for b in range(visits):
+        right, left = blocks[min(b + 1, visits - 1)], blocks[max(b - 1, 0)]
+        packs[b] = pack(jnp.where(lane < LANES // 2, right, left), -LANES // groups // 2)
+        pl.when(me > b + 1)(lambda b=b: send_windows(jnp.int32(b), (-1, 0)))
+    own = tiles[1].astype(F32)
+    tile_packs[0] = pack(own, 0)
+    tile_packs[1] = pack(own, LANES - LANES // groups)
     pl.when(above)(lambda: send_row(-1))
-    send_ahead((-1, 0))
+    send_next_ahead((-1, 0))
 
     windows[me, main:main + groups] = image[:, :, pl.ds(pl.multiple_of(me * LANES, LANES), LANES)]
     windows[me, main + groups] = packs[me]
@@ -292,7 +300,7 @@
     for b in range(3, visits):
         pl.when(me + 2 < b)(lambda b=b: send_far(jnp.int32(b)))
 
-    await_tiles(got_tiles)
+    await_blocks(got_tiles.at[0], tile_blocks)
     lane = lax.broadcasted_iota(jnp.int32, (in_rows, LANES), 1)
     every, width = range(groups), LANES // groups
     centre = tiles[...].astype(F32).reshape(in_rows, LANES)
@@ -362,9 +370,7 @@
     psf_high, psf_low = cols_high[BASES, :, :LANES], cols_low[BASES, :, :LANES]
     filtered = mm(high, psf_high) + (mm(high, psf_low) + mm(low, psf_high))
     out[...] = filtered / jnp.full(filtered.shape, denominator, F32)
-    await_tiles(sent_tiles)
-    for b in range(visits):
-        await_windows(sent_windows, jnp.int32(b))
+    await_blocks(sent.at[0], sent_blocks)
 
 
 def solution(mesh):
@@ -374,6 +380,9 @@
     def shards(template, images, basis_taps, psf_taps, coeffs, offsets, cover, weights):
         slab_rows = template.shape[0]
         images = images.reshape(images.shape[0], slab_rows // 8, 8, images.shape[2])
+        groups, halo = slab_rows // 8, HALO // 8
+        sent = 2 * groups + 6 + (visits - 1) * (groups + 1) + 2 * visits * (halo + 1)
+        sent = max(sent, groups * (1 + images.shape[3] // LANES))
         vmem = pl.BlockSpec(memory_space=pltpu.VMEM)
         small = (
             basis_taps, psf_taps, coeffs.transpose(1, 0, 2), offsets.transpose(1, 0), cover, weights
@@ -393,10 +402,10 @@
                 pltpu.VMEM((2, 3, 8, LANES), BF16),
                 pltpu.VMEM((BASES + 1, WIDE, WIDE), BF16),
                 pltpu.VMEM((BASES + 1, WIDE, WIDE), BF16),
-                pltpu.SemaphoreType.DMA((8,)),
-                pltpu.SemaphoreType.DMA((3,)),
-                pltpu.SemaphoreType.DMA((3,)),
-                pltpu.SemaphoreType.DMA((visits,)),
+                pltpu.SemaphoreType.DMA((2,)),
+                pltpu.VMEM((sent, 8, LANES), BF16),
+                pltpu.SemaphoreType.DMA((1,)),
+                pltpu.SemaphoreType.DMA((1,)),
                 pltpu.SemaphoreType.DMA((visits,)),
                 pltpu.SemaphoreType.REGULAR((visits,)),
             ],

time: 9.27 us -> 9.06 us (0.977)
  Pallas kernels: 8.47 us -> 8.26 us
    pallas_call x1, Pallas kernels: 8.47 us -> 8.26 us  [shards(): pl.pallas_call(functools.partial(kernel, (visits, slabs, bands)), out_sha...]
where the time goes in v2:
time: 9.06 us; the launch traced here: 8.88 us
  Pallas kernels  8.26 us (91%)
  local copies, waits for them, and re-layouts  0.61 us (7%)
    pallas_call x1, Pallas kernels, shards(): pl.pallas_call(functools.partial(kernel, (visits, slabs, bands)), out_sha...  8.26 us
    unnamed x1, local copies, waits for them, and re-layouts  0.61 us

profile of v2, /device:TPU:1, one launch (start us, length us, event | category | flops | bytes accessed | tf_op | source)
XLA Modules:
  0.0 8.9 jit_solution(13726311347092885337)
XLA Ops:
  0.0 8.3 %coadd.1 = f32[32,128]{1,0:T(8,128)S(1)} custom-call(bf16[32,128]{1,0:T(8,128)(2,1)} %template.1, bf16[1,4,8,512]{3,2,1,0:T(8,128)(2,1)} %bitcast.3, f32[3,19]{1,0:T(4,128)} %small_0_.1, f32[2,19]{1,0:T(2,128)} %small_1_.1, f32[3,4,6]{2,1,0:T(4,128)} %bitcast.4, s32[2,4]{1,0:T(2,128)} %bitcast.5, s32[4,4]{1,0:T(4,128)} %small_4_.1, f32[4]{0:T(128)} %small_5_.1), custom_call_target="tpu_custom_call" | custom-call | tf_op jit(solution)/shard_map/coadd/pallas_call | solution.py:390
  8.3 0.6 %copy.10 = f32[32,128]{1,0:T(8,128)} copy(f32[32,128]{1,0:T(8,128)S(1)} %coadd.1) | data formatting | bytes 32768
